TPU v7x, 32 devices: a whole 2x2x4 slice. The times are simulated.
32 devices in a mesh: groups: 2 (over x), ctx: 16 (over z, y, core).
Axes of the slice: x: 2, y: 2, z: 4, core: 2. Of those that a mesh axis runs over, the one named last changes fastest.
Arguments:
- hidden_in: bfloat16 [4096, 2048], P(('groups', 'ctx')), parts along dimension 0, may hold values from -6 to 6
- span_order: int32 [32, 2], P('groups'), parts along dimension 0, may hold values from 0 to 31, as said below
- norm_gain: float32 [2048], replicated, may hold values from 0.5 to 1.5
- w_query: bfloat16 [2048, 2048], replicated, may hold values from -0.125 to 0.125
- w_key: bfloat16 [2048, 256], replicated, may hold values from -0.125 to 0.125
- w_value: bfloat16 [2048, 256], replicated, may hold values from -0.125 to 0.125
- query_gain: float32 [128], replicated, may hold values from 1.5 to 7
- key_gain: float32 [128], replicated, may hold values from 1.5 to 7
Outputs:
- attended: bfloat16 [4096, 2048], P(('groups', 'ctx')), parts along dimension 0
There are 2 independent parts, one for each index of `groups`. A program takes and returns all parts, laid end to end along the dimension named above; an argument that names none is the same for every part. Nothing has to cross between parts.
Inputs may be any that keep to these rules, and one draw needn't show every extreme that they name: `span_order`: row d holds a span c and the span 2 * 16 - 1 - c with c < 16; the rows together name every span once; a device's first 64 rows are its column 0 span.
All inputs are finite; a program needn't handle non-finite values.
Results may differ from a plain program's by a relative error of at most 0.0075.
The roundings to bfloat16 on the way count: a program that leaves them out, or rounds other values in their place, can miss the bound.
Values may be sent and summed in bfloat16 or wider, within the bound.
No kernel may reach another device: no remote copies, remote signals or barrier semaphores. Data moves between devices by JAX's collectives and lax.ppermute only.
A program may use at most 128 MiB of HBM per device.

v0:
```python
import functools
import math

import jax
import jax.numpy as jnp
import numpy as np
from jax import lax
from jax.experimental import pallas as pl
from jax.experimental.pallas import tpu as pltpu
from jax.sharding import PartitionSpec as P


HEADS = 16
KV_HEADS = 2
HEAD = 128
GROUP = HEADS // KV_HEADS
EPSILON = 1e-06
THETA = 1000000.0
SCALE = HEAD**-0.5 * math.log2(math.e)
HIDDEN = -1e30
UNIT = 4
TILE = 512


VMEM = pltpu.VMEM
SMEM = pltpu.SMEM
F32 = jnp.float32
BF16 = jnp.bfloat16
DMA = pltpu.SemaphoreType.DMA


def placed(space):
    return pl.BlockSpec(memory_space=space)


def partner(x, offset):
    return lax.ppermute(x, "ctx", [(i, i ^ offset) for i in range(lax.axis_size("ctx"))])


def table(half, spans):
    inverse = THETA ** -(2.0 * np.arange(HEAD // 2) / HEAD)
    inverse = np.concatenate([inverse, inverse])[None, :]
    within = np.arange(half)[:, None] * inverse
    start = (np.arange(spans) * half)[:, None] * inverse
    return jnp.asarray(np.concatenate([np.cos(within), np.sin(within), np.cos(start), np.sin(start)]), F32)


def rope(entries, cosine, sine):
    square = entries * entries
    high = square.astype(BF16)
    low = (square - high.astype(F32)).astype(BF16)
    mean = jnp.full((HEAD, HEAD), 1.0 / HEAD, BF16)
    mean_square = jnp.dot(high, mean, preferred_element_type=F32) + jnp.dot(low, mean, preferred_element_type=F32)
    turned = entries * cosine + pltpu.roll(entries, HEAD // 2, 1) * sine
    return turned * lax.rsqrt(mean_square + EPSILON)


def gained(gain, angles):
    lane = lax.broadcasted_iota(jnp.int32, (angles.shape[0], HEAD), 1)
    cosine, sine = angles[:, :HEAD], angles[:, HEAD:]
    signed = jnp.where(lane < HEAD // 2, -sine, sine)
    return cosine * gain, signed * pltpu.roll(gain, HEAD // 2, 1)


def start_all(copies):
    copies = [pltpu.make_async_copy(*copy) for copy in copies]
    for copy in copies:
        copy.start()
    return copies


def key_value_kernel(
    spans_in, hidden_in, norm_gain_in, w_key_in, w_value_in, key_gain_in, query_gain_in, table_in, shared_out, kv_out,
    spans, hidden, norm_gain, w_key, w_value, key_gain, query_gain, steps, shared, angles, sems,
):
    width = hidden.shape[1]
    got_hidden, got_norm_gain, got_spans, got_steps, got_key_gain, got_query_gain, got_key, got_value = start_all(
        [
            (hidden_in, hidden, sems.at[0]),
            (norm_gain_in, norm_gain, sems.at[1]),
            (spans_in, spans, sems.at[2]),
            (table_in, steps, sems.at[3]),
            (key_gain_in, key_gain, sems.at[4]),
            (query_gain_in, query_gain, sems.at[5]),
            (w_key_in, w_key, sems.at[6]),
            (w_value_in, w_value, sems.at[7]),
        ]
    )
    own = lax.axis_index("ctx")
    half = hidden.shape[0] // 2
    count = (steps.shape[0] - 2 * half) // 2
    got_spans.wait()
    got_steps.wait()
    for part in range(2):
        span = spans[part, own]
        cos_a, sin_a = steps[pl.ds(2 * half + span, 1), :], steps[pl.ds(2 * half + count + span, 1), :]
        cos_b, sin_b = steps[:half], steps[half : 2 * half]
        rows = pl.ds(part * half, half)
        angles[rows, :HEAD] = cos_a * cos_b - sin_a * sin_b
        angles[rows, HEAD:] = sin_a * cos_b + cos_a * sin_b
    got_query_gain.wait()
    for part, turn in enumerate(gained(query_gain[...], angles[...])):
        for piece in range(3):
            column = width + (3 * part + piece) * HEAD
            rounded = turn.astype(BF16)
            shared[:, column : column + HEAD] = rounded
            turn = turn - rounded.astype(F32)
    got_hidden.wait()
    got_norm_gain.wait()
    entries = hidden[...].astype(F32)
    mean_square = jnp.mean(entries * entries, axis=-1, keepdims=True)
    shared[:, :width] = (entries * lax.rsqrt(mean_square + EPSILON) * norm_gain[...]).astype(BF16)
    put_shared = pltpu.make_async_copy(shared, shared_out, sems.at[0])
    put_shared.start()
    got_key_gain.wait()
    cosine, sine = gained(key_gain[...], angles[...])
    got_key.wait()
    keys = jnp.dot(shared[:, :width], w_key[...], preferred_element_type=F32)
    got_value.wait()
    for head in range(KV_HEADS):
        columns = slice(head * HEAD, (head + 1) * HEAD)
        kv_out[:, columns] = rope(keys[:, columns], cosine, sine).astype(BF16)
    values = jnp.dot(shared[:, :width], w_value[...], preferred_element_type=F32)
    kv_out[:, KV_HEADS * HEAD :] = values.astype(BF16)
    put_shared.wait()


def query_kernel(shared_in, w_query, out, shared, weights, product, sems):
    tiles, width, _ = weights.shape
    got_shared, *got = start_all(
        [(shared_in, shared, sems.at[0])]
        + [(w_query.at[:, pl.ds(i * TILE, TILE)], weights.at[i], sems.at[1 + i]) for i in range(tiles)]
    )
    got_shared.wait()
    pieces = [shared[:, width + i * HEAD : width + (i + 1) * HEAD].astype(F32) for i in range(6)]
    cosine, sine = (pieces[i] + pieces[i + 1] + pieces[i + 2] for i in (0, 3))
    for index in range(tiles + 1):
        if index < tiles:
            got[index].wait()
            product[index % 2] = jnp.dot(shared[:, :width], weights[index], preferred_element_type=F32)
        if index > 0:
            for head in range(TILE // HEAD):
                column = (index - 1) * TILE + head * HEAD
                entries = product[(index - 1) % 2][:, head * HEAD : (head + 1) * HEAD]
                out[:, column : column + HEAD] = rope(entries, cosine, sine).astype(BF16)


def unit_count(blocks, own):
    seen = blocks + 1 if own else blocks
    return max(-(-e // UNIT) - (-(seen - e) // UNIT) for e in range(1 if own else 0, blocks + 1))


def attention_kernel(devices, offsets, first, last, spans, queries, *refs):
    blocks = sum(len(group) for group in offsets)
    pieces, refs = refs[: len(offsets)], refs[len(offsets) :]
    if not first:
        (peak_in, total_in, accum_in), refs = refs[:3], refs[3:]
    if last:
        out, peak, total, accum, kv, scores_a, scores_b, packed, sem = refs
    else:
        peak, total, accum, kv, scores_a, scores_b, packed, sem = refs
    has_own = offsets[0][0] == 0
    own = lax.axis_index("ctx")
    half = queries.shape[0] // 2
    lanes = GROUP * half
    part_rows = kv.shape[0] // 2
    unit = UNIT * half

    def early_of(device):
        return jnp.minimum(spans[0, device], spans[1, device])

    def rows_in(device, base=0):
        row = jnp.where(spans[0, device] < spans[1, device], 0, half)
        return [pl.ds(pl.multiple_of(base + r, half), half) for r in (row, half - row)]

    mine = early_of(own)
    if blocks == devices:

        def fetch(piece, base, source):
            rank = early_of(source)
            for rows, at in zip(rows_in(source, base), (rank, 2 * blocks - 1 - rank)):
                to = pl.ds(pl.multiple_of(at * half, half), half)
                pltpu.make_async_copy(piece.at[rows, :], kv.at[to, :], sem).start()

        for piece, group in zip(pieces, offsets):

            @pl.loop(0, len(group))
            def _(index, piece=piece, group=group):
                fetch(piece, index * 2 * half, own ^ (group[0] + index))

        pltpu.make_async_copy(kv, kv, sem).wait()
        early_seen, late_seen = mine + 1, blocks - mine
    else:
        sources = [own ^ group[0] for group in offsets]
        early = [early_of(source) for source in sources]
        early_seen = sum((e <= mine).astype(jnp.int32) for e in early)
        late_seen = sum((e >= mine).astype(jnp.int32) for e in early)
        for part in range(2):
            if part_rows > blocks * half:
                pad = pl.ds(part * part_rows + blocks * half, part_rows - blocks * half)
                kv[pad, :] = jnp.zeros((part_rows - blocks * half, kv.shape[1]), BF16)
        for piece, source, e in zip(pieces, sources, early):
            rank = sum((other < e).astype(jnp.int32) for other in early)
            for rows, at in zip(rows_in(source), (rank * half, part_rows + (blocks - 1 - rank) * half)):
                kv[pl.ds(pl.multiple_of(at, half), half), :] = piece[rows, :]

    early_units = (early_seen + UNIT - 1) // UNIT
    a_steps = [(row, min(unit, blocks * half - row)) for row in range(0, blocks * half, unit)]
    b_units = unit_count(blocks, has_own)
    query_rows = rows_in(own)

    def each(count, step):
        if count <= 8:
            for index in range(count):
                step(index)
        else:
            pl.loop(0, count)(step)

    def a_rows(index):
        if len(a_steps) <= 8:
            return pl.ds(*a_steps[index])
        return pl.ds(pl.multiple_of(index * unit, unit), unit)

    def b_unit(index):
        late = jnp.where(index < early_units, 0, 1)
        start = jnp.where(index < early_units, index, index - early_units) * unit
        row = late * part_rows + jnp.minimum(start, part_rows - unit)
        seen = jnp.where(late == 1, late_seen, early_seen)
        return late, start - (seen - 1) * half, pl.ds(pl.multiple_of(row, half), unit)

    def b_rows(index):
        return pl.ds(index * unit if isinstance(index, int) else pl.multiple_of(index * unit, unit), unit)

    def slot(head):
        return head % scores_a.shape[0]

    def folded(x, reduce):
        return reduce(x.reshape(x.shape[0] // 8, 8, x.shape[1]), axis=0)

    def spread(x, reduce):
        return jnp.broadcast_to(reduce(x, axis=0, keepdims=True), (8, lanes))

    def score(head, rows, late):
        return lax.dot_general(
            kv[rows, pl.ds(head * HEAD, HEAD)], packed[head, late], (((1,), (1,)), ((), ())), preferred_element_type=F32
        )

    def find_scores(head):
        for late in range(2):
            for g in range(GROUP):
                column = (head * GROUP + g) * HEAD
                packed[head, late, g * half : (g + 1) * half, :] = queries[query_rows[late], column : column + HEAD]
            if first:
                peak[head, late] = jnp.full((8, lanes), HIDDEN, F32)
            else:
                peak[head, late] = peak_in[head, late]

        def step_a(index):
            scores = score(head, a_rows(index), 1)
            scores_a[slot(head), a_rows(index), :] = scores
            peak[head, 1] = jnp.maximum(peak[head, 1], folded(scores, jnp.max))

        def step_b(index):
            late, ahead, rows = b_unit(index)
            scores = score(head, rows, late)
            key_at = ahead + lax.broadcasted_iota(jnp.int32, scores.shape, 0)
            query_at = lax.broadcasted_iota(jnp.int32, scores.shape, 1) % half if has_own else half - 1
            scores = jnp.where(key_at <= query_at, scores, HIDDEN)
            scores_b[slot(head), b_rows(index), :] = scores
            peak[head, late] = jnp.maximum(peak[head, late], folded(scores, jnp.max))

        each(len(a_steps), step_a)
        each(b_units, step_b)

    def blend(head):
        for late in range(2):
            peak[head, late] = spread(peak[head, late], jnp.max)
            if first:
                total[head, late] = jnp.zeros((8, lanes), F32)
                accum[head, late] = jnp.zeros((HEAD, lanes), F32)
            else:
                decay = jnp.exp2((peak_in[head, late] - peak[head, late]) * SCALE)
                total[head, late] = total_in[head, late] * decay
                accum[head, late] = accum_in[head, late] * decay[:1]

        def add(scores, late, rows):
            weights = jnp.exp2((scores - peak[head, late][:1]) * SCALE)
            total[head, late] += folded(weights, jnp.sum)
            accum[head, late] += lax.dot_general(
                kv[rows, pl.ds((KV_HEADS + head) * HEAD, HEAD)],
                weights.astype(BF16),
                (((0,), (0,)), ((), ())),
                preferred_element_type=F32,
            )

        def step_a(index):
            add(scores_a[slot(head), a_rows(index), :], 1, a_rows(index))

        def step_b(index):
            late, _, rows = b_unit(index)
            add(scores_b[slot(head), b_rows(index), :], late, rows)

        each(len(a_steps), step_a)
        each(b_units, step_b)
        if last:
            for late in range(2):
                blended = accum[head, late] / jnp.sum(total[head, late], axis=0, keepdims=True)
                blended = blended.T.astype(BF16)
                for g in range(GROUP):
                    column = (head * GROUP + g) * HEAD
                    out[query_rows[late], column : column + HEAD] = blended[g * half : (g + 1) * half]

    for step in (find_scores, blend) if scores_a.shape[0] == KV_HEADS else (lambda head: (find_scores(head), blend(head)),):
        for head in range(KV_HEADS):
            step(head)


def attend(devices, offsets, spans, queries, pieces, state=(), last=True):
    rows = queries.shape[0]
    half = rows // 2
    lanes = GROUP * half
    blocks = sum(len(group) for group in offsets)
    part_rows = -(-blocks // UNIT) * UNIT * half
    b_rows = unit_count(blocks, offsets[0][0] == 0) * UNIT * half
    shapes = [(KV_HEADS, 2, 8, lanes), (KV_HEADS, 2, 8, lanes), (KV_HEADS, 2, HEAD, lanes)]
    states = [VMEM(shape, F32) for shape in shapes]
    relayed = len(offsets) == blocks
    slots = KV_HEADS if relayed else 1
    if last:
        out_shape, out_specs = jax.ShapeDtypeStruct((rows, HEADS * HEAD), BF16), placed(VMEM)
    else:
        out_shape, out_specs = [jax.ShapeDtypeStruct(shape, F32) for shape in shapes], [placed(VMEM)] * 3
    return pl.pallas_call(
        functools.partial(attention_kernel, devices, offsets, not state, last),
        out_shape=out_shape,
        in_specs=[placed(SMEM), placed(VMEM)]
        + [placed(VMEM if relayed else pl.ANY)] * len(pieces)
        + [placed(VMEM)] * len(state),
        out_specs=out_specs,
        scratch_shapes=(states if last else [])
        + [
            VMEM((2 * part_rows, pieces[0].shape[1]), BF16),
            VMEM((slots, blocks * half, lanes), F32),
            VMEM((slots, b_rows, lanes), F32),
            VMEM((KV_HEADS, 2, lanes, HEAD), BF16),
            DMA,
        ],
        compiler_params=pltpu.CompilerParams(vmem_limit_bytes=(20 if relayed else 63) << 20),
        cost_estimate=pl.CostEstimate(
            flops=8 * rows * rows * blocks * HEADS * HEAD // 2, bytes_accessed=2 * rows * HEADS * HEAD, transcendentals=0
        ),
        name="attention",
    )(spans, queries, *pieces, *state)


def body(hidden_in, span_order, norm_gain, w_query, w_key, w_value, query_gain, key_gain):
    rows, width = hidden_in.shape
    half = rows // 2
    devices = lax.axis_size("ctx")
    kv_width = 2 * KV_HEADS * HEAD
    steps = table(half, 2 * devices)
    span_order = span_order.T

    shared_width = width + 6 * HEAD
    shared, kv = pl.pallas_call(
        key_value_kernel,
        out_shape=(jax.ShapeDtypeStruct((rows, shared_width), BF16), jax.ShapeDtypeStruct((rows, kv_width), BF16)),
        in_specs=[placed(pl.ANY)] * 8,
        out_specs=[placed(pl.ANY), placed(VMEM)],
        scratch_shapes=[
            SMEM(span_order.shape, jnp.int32),
            VMEM((rows, width), BF16),
            VMEM((1, width), F32),
            VMEM(w_key.shape, BF16),
            VMEM(w_value.shape, BF16),
            VMEM((1, HEAD), F32),
            VMEM((1, HEAD), F32),
            VMEM(steps.shape, F32),
            VMEM((rows, shared_width), BF16),
            VMEM((rows, 2 * HEAD), F32),
            DMA((8,)),
        ],
        compiler_params=pltpu.CompilerParams(vmem_limit_bytes=63 << 20),
        name="key_value",
    )(
        span_order,
        hidden_in,
        norm_gain.reshape(1, width),
        w_key,
        w_value,
        key_gain.reshape(1, HEAD),
        query_gain.reshape(1, HEAD),
        steps,
    )

    tiles = HEADS * HEAD // TILE
    queries = pl.pallas_call(
        query_kernel,
        out_shape=jax.ShapeDtypeStruct((rows, HEADS * HEAD), BF16),
        in_specs=[placed(pl.ANY)] * 2,
        out_specs=placed(VMEM),
        scratch_shapes=[
            VMEM((rows, shared_width), BF16),
            VMEM((tiles, width, TILE), BF16),
            VMEM((2, rows, TILE), F32),
            DMA((1 + tiles,)),
        ],
        compiler_params=pltpu.CompilerParams(vmem_limit_bytes=53 << 20),
        cost_estimate=pl.CostEstimate(
            flops=2 * rows * width * HEADS * HEAD, bytes_accessed=2 * width * HEADS * HEAD, transcendentals=0
        ),
        name="query",
    )(shared, w_query)

    far = devices // 2
    if devices > 16:
        held, count = kv, 1
        while count < far:
            held = jnp.concatenate([held, partner(held, count)])
            count *= 2
        pieces, offsets = [held, partner(held, far)], [list(range(far)), list(range(far, devices))]
        return attend(devices, offsets, span_order, queries, pieces)

    def cores(pieces):
        for offset in list(pieces):
            pieces[offset + 1] = partner(pieces[offset], 1)
        return [[offset] for offset in pieces], list(pieces.values())

    near = range(2, far, 2)
    pieces = {0: kv, far: partner(kv, far)}
    for offset in near:
        pieces[offset] = partner(kv, offset)
    relayed = {}
    for offset in near:
        relayed[far + offset] = partner(pieces[far], offset)
    offsets, pieces = cores(pieces)
    state = attend(devices, offsets, span_order, queries, pieces, last=False)
    offsets, pieces = cores(relayed)
    return attend(devices, offsets, span_order, queries, pieces, state)


def solution(mesh):
    in_specs = (P(("groups", "ctx"), None), P("groups", None), P(), P(), P(), P(), P(), P())
    out_specs = P(("groups", "ctx"), None)
    return jax.shard_map(body, mesh=mesh, in_specs=in_specs, out_specs=out_specs, check_vma=False)
```

profile of v0, /device:TPU:0, one launch (start us, length us, event | category | flops | bytes accessed | tf_op | source)
XLA Modules:
  0.0 38.2 jit_solution(17893841941257409954)
XLA Ops:
  0.0 0.0 copy-start
  0.0 3.1 %key_value.1 = (bf16[128,2816]{1,0:T(8,128)(2,1)}, bf16[128,512]{1,0:T(8,128)(2,1)}) custom-call(s32[2,16]{1,0:T(2,128)} %bitcast.4, bf16[128,2048]{1,0:T(8,128)(2,1)} %hidden_in.1, f32[1,2048]{1,0:T(1,128)} %bitcast.7, bf16[2048,256]{1,0:T(8,128)(2,1)} %w_key_in.1, bf16[2048,256]{1,0:T(8,128)(2,1)} %w_value_in.1, f32[1,128]{1,0:T(1,128)} %bitcast.8, ...), custom_call_target="tpu_custom_call" | custom-call | tf_op jit(solution)/shard_map/key_value/pallas_call | solution.py:365
  3.1 0.0 copy-start.1
  3.1 4.1 %collective-permute-start.9 = (bf16[128,512]{1,0:T(8,128)(2,1)}, bf16[128,512]{1,0:T(8,128)(2,1)S(1)}, u32[]{:S(2)}, u32[]{:S(2)}) collective-permute-start(bf16[128,512]{1,0:T(8,128)(2,1)} %get-tuple-element.11.refs_0_), channel_id=1, source_target_pairs={{0,6},{1,7},{2,4},{3,5},{4,2},{5,3},{6,0},{7,1},{8,14},{9,15},{10,... | collective-permute-start | bytes 393224 | tf_op jit(solution)/shard_map/ppermute | solution.py:37
  7.2 0.5 %collective-permute-start.8 = (bf16[128,512]{1,0:T(8,128)(2,1)}, bf16[128,512]{1,0:T(8,128)(2,1)S(1)}, u32[]{:S(2)}, u32[]{:S(2)}) collective-permute-start(bf16[128,512]{1,0:T(8,128)(2,1)} %get-tuple-element.11.refs_0_), channel_id=1, source_target_pairs={{0,4},{1,5},{2,6},{3,7},{4,0},{5,1},{6,2},{7,3},{8,12},{9,13},{10,... | collective-permute-start | bytes 393224 | tf_op jit(solution)/shard_map/ppermute | solution.py:37
  7.6 2.6 %collective-permute-start = (bf16[128,512]{1,0:T(8,128)(2,1)}, bf16[128,512]{1,0:T(8,128)(2,1)S(1)}, u32[]{:S(2)}, u32[]{:S(2)}) collective-permute-start(bf16[128,512]{1,0:T(8,128)(2,1)} %get-tuple-element.11.refs_0_), channel_id=1, source_target_pairs={{0,8},{1,9},{2,10},{3,11},{4,12},{5,13},{6,14},{7,15},{8,0},{9,1},... | collective-permute-start | bytes 393224 | tf_op jit(solution)/shard_map/ppermute | solution.py:37
  10.2 0.0 collective-permute-start.10
  10.2 0.5 %collective-permute-start.7 = (bf16[128,512]{1,0:T(8,128)(2,1)}, bf16[128,512]{1,0:T(8,128)(2,1)S(1)}, u32[]{:S(2)}, u32[]{:S(2)}) collective-permute-start(bf16[128,512]{1,0:T(8,128)(2,1)} %get-tuple-element.11.refs_0_), channel_id=1, source_target_pairs={{0,2},{1,3},{2,0},{3,1},{4,6},{5,7},{6,4},{7,5},{8,10},{9,11},{10,... | collective-permute-start | bytes 393224 | tf_op jit(solution)/shard_map/ppermute | solution.py:37
  10.7 3.8 %collective-permute-done.9.refs_4_ = bf16[128,512]{1,0:T(8,128)(2,1)S(1)} collective-permute-done((bf16[128,512]{1,0:T(8,128)(2,1)}, bf16[128,512]{1,0:T(8,128)(2,1)S(1)}, u32[]{:S(2)}, u32[]{:S(2)}) %collective-permute-start.9) | collective-permute-done | bytes 131104 | tf_op jit(solution)/shard_map/ppermute | solution.py:37
  14.6 0.0 collective-permute-start.14
  14.6 2.1 %collective-permute-done.8.refs_3_ = bf16[128,512]{1,0:T(8,128)(2,1)S(1)} collective-permute-done((bf16[128,512]{1,0:T(8,128)(2,1)}, bf16[128,512]{1,0:T(8,128)(2,1)S(1)}, u32[]{:S(2)}, u32[]{:S(2)}) %collective-permute-start.8) | collective-permute-done | bytes 131104 | tf_op jit(solution)/shard_map/ppermute | solution.py:37
  16.7 0.0 collective-permute-start.13
  16.7 0.0 collective-permute-done.refs_1_
  16.7 2.5 %collective-permute-start.3 = (bf16[128,512]{1,0:T(8,128)(2,1)S(1)}, bf16[128,512]{1,0:T(8,128)(2,1)S(1)}, u32[]{:S(2)}, u32[]{:S(2)}) collective-permute-start(bf16[128,512]{1,0:T(8,128)(2,1)S(1)} %collective-permute-done.refs_1_), channel_id=1, source_target_pairs={{0,6},{1,7},{2,4},{3,5},{4,2},{5,3},{6,0},{7,1},{8,14},{9,15},{10,... | collective-permute-start | bytes 393224 | tf_op jit(solution)/shard_map/ppermute | solution.py:37
  19.2 0.0 collective-permute-done.10.refs_5_
  19.2 0.1 collective-permute-start.2
  19.3 0.0 collective-permute-done.7.refs_2_
  19.3 1.5 %collective-permute-start.1 = (bf16[128,512]{1,0:T(8,128)(2,1)S(1)}, bf16[128,512]{1,0:T(8,128)(2,1)S(1)}, u32[]{:S(2)}, u32[]{:S(2)}) collective-permute-start(bf16[128,512]{1,0:T(8,128)(2,1)S(1)} %collective-permute-done.refs_1_), channel_id=1, source_target_pairs={{0,2},{1,3},{2,0},{3,1},{4,6},{5,7},{6,4},{7,5},{8,10},{9,11},{10,... | collective-permute-start | bytes 393224 | tf_op jit(solution)/shard_map/ppermute | solution.py:37
  20.8 0.0 collective-permute-done.14.refs_9_
  20.8 0.0 collective-permute-start.12
  20.8 0.0 collective-permute-done.13.refs_8_
  20.8 0.5 %collective-permute-start.11 = (bf16[128,512]{1,0:T(8,128)(2,1)S(1)}, bf16[128,512]{1,0:T(8,128)(2,1)S(1)}, u32[]{:S(2)}, u32[]{:S(2)}) collective-permute-start(bf16[128,512]{1,0:T(8,128)(2,1)S(1)} %collective-permute-done.refs_1_), channel_id=1, source_target_pairs={{0,1},{1,0},{2,3},{3,2},{4,5},{5,4},{6,7},{7,6},{8,9},{9,8},{10,11... | collective-permute-start | bytes 393224 | tf_op jit(solution)/shard_map/ppermute | solution.py:37
  21.3 2.7 %collective-permute-done.3.refs_2_ = bf16[128,512]{1,0:T(8,128)(2,1)S(1)} collective-permute-done((bf16[128,512]{1,0:T(8,128)(2,1)S(1)}, bf16[128,512]{1,0:T(8,128)(2,1)S(1)}, u32[]{:S(2)}, u32[]{:S(2)}) %collective-permute-start.3) | collective-permute-done | bytes 131104 | tf_op jit(solution)/shard_map/ppermute | solution.py:37
  24.0 0.0 collective-permute-start.6
  24.0 1.2 %collective-permute-done.2.refs_1_ = bf16[128,512]{1,0:T(8,128)(2,1)S(1)} collective-permute-done((bf16[128,512]{1,0:T(8,128)(2,1)S(1)}, bf16[128,512]{1,0:T(8,128)(2,1)S(1)}, u32[]{:S(2)}, u32[]{:S(2)}) %collective-permute-start.2) | collective-permute-done | bytes 131104 | tf_op jit(solution)/shard_map/ppermute | solution.py:37
  25.2 0.0 collective-permute-start.5
  25.2 1.1 %collective-permute-done.1.refs_0_ = bf16[128,512]{1,0:T(8,128)(2,1)S(1)} collective-permute-done((bf16[128,512]{1,0:T(8,128)(2,1)S(1)}, bf16[128,512]{1,0:T(8,128)(2,1)S(1)}, u32[]{:S(2)}, u32[]{:S(2)}) %collective-permute-start.1) | collective-permute-done | bytes 131104 | tf_op jit(solution)/shard_map/ppermute | solution.py:37
  26.3 0.0 collective-permute-start.4
  26.3 4.4 %query.1.queries = bf16[128,2048]{1,0:T(8,128)(2,1)S(1)} custom-call(bf16[128,2816]{1,0:T(8,128)(2,1)} %get-tuple-element.10.shared_in, bf16[2048,2048]{1,0:T(8,128)(2,1)} %w_query.1), custom_call_target="tpu_custom_call" | custom-call | flops 1073741824 | bytes 8388608 | tf_op jit(solution)/shard_map/query/pallas_call | solution.py:397
  30.8 0.0 collective-permute-done.12.refs_7_
  30.8 0.0 collective-permute-done.11.refs_6_
  30.8 0.0 copy-done
  30.8 0.0 copy-done.1
  30.8 3.6 %attention.2 = (f32[2,2,8,512]{3,2,1,0:T(8,128)S(1)}, f32[2,2,8,512]{3,2,1,0:T(8,128)S(1)}, f32[2,2,128,512]{3,2,1,0:T(8,128)S(1)}) custom-call(s32[2,16]{1,0:T(2,128)S(1)} %bitcast.5, bf16[128,2048]{1,0:T(8,128)(2,1)S(1)} %query.1.queries, bf16[128,512]{1,0:T(8,128)(2,1)S(1)} %copy-done.1, bf16[128,512]{1,0:T(8,128)(2,1)S(1)} %collective-permute-done.refs_1_, ...), custom_call_target="tpu_custom_call" | custom-call | flops 1342177280 | bytes 524288 | tf_op jit(solution)/shard_map/attention/pallas_call | solution.py:333
  34.4 0.0 collective-permute-done.6.refs_5_
  34.4 0.0 collective-permute-done.5.refs_4_
  34.4 0.0 collective-permute-done.4.refs_3_
  34.4 3.8 %attention.3 = bf16[128,2048]{1,0:T(8,128)(2,1)} custom-call(s32[2,16]{1,0:T(2,128)S(1)} %bitcast.6, bf16[128,2048]{1,0:T(8,128)(2,1)S(1)} %query.1.queries, bf16[128,512]{1,0:T(8,128)(2,1)S(1)} %collective-permute-done.1.refs_0_, bf16[128,512]{1,0:T(8,128)(2,1)S(1)} %collective-permute-done.2.refs_1_, bf16[128,512]{1,0:T(8,128)(2,1)S(1)} %collective-permute-done.3.refs_2_, ...), custom_call_target="tpu_custom_call" | custom-call | flops 805306368 | bytes 524288 | tf_op jit(solution)/shard_map/attention/pallas_call | solution.py:333
Async XLA Ops:
  0.0 30.8 %copy-start = (s32[16,2]{0,1:T(2,128)S(1)}, s32[16,2]{0,1:T(2,128)}, u32[]{:S(2)}) copy-start(s32[16,2]{0,1:T(2,128)} %param.10) | copy-start | bytes 388
  3.1 27.7 %copy-start.1 = (bf16[128,512]{1,0:T(8,128)(2,1)S(1)}, bf16[128,512]{1,0:T(8,128)(2,1)}, u32[]{:S(2)}) copy-start(bf16[128,512]{1,0:T(8,128)(2,1)} %get-tuple-element.11.refs_0_) | copy-start | bytes 393220
  3.1 11.4 %collective-permute-start.9 = (bf16[128,512]{1,0:T(8,128)(2,1)}, bf16[128,512]{1,0:T(8,128)(2,1)S(1)}, u32[]{:S(2)}, u32[]{:S(2)}) collective-permute-start(bf16[128,512]{1,0:T(8,128)(2,1)} %get-tuple-element.11.refs_0_), channel_id=1, source_target_pairs={{0,6},{1,7},{2,4},{3,5},{4,2},{5,3},{6,0},{7,1},{8,14},{9,15},{10,... | collective-permute-start | bytes 393224 | tf_op jit(solution)/shard_map/ppermute | solution.py:37
  7.2 9.5 %collective-permute-start.8 = (bf16[128,512]{1,0:T(8,128)(2,1)}, bf16[128,512]{1,0:T(8,128)(2,1)S(1)}, u32[]{:S(2)}, u32[]{:S(2)}) collective-permute-start(bf16[128,512]{1,0:T(8,128)(2,1)} %get-tuple-element.11.refs_0_), channel_id=1, source_target_pairs={{0,4},{1,5},{2,6},{3,7},{4,0},{5,1},{6,2},{7,3},{8,12},{9,13},{10,... | collective-permute-start | bytes 393224 | tf_op jit(solution)/shard_map/ppermute | solution.py:37
  7.6 9.0 %collective-permute-start = (bf16[128,512]{1,0:T(8,128)(2,1)}, bf16[128,512]{1,0:T(8,128)(2,1)S(1)}, u32[]{:S(2)}, u32[]{:S(2)}) collective-permute-start(bf16[128,512]{1,0:T(8,128)(2,1)} %get-tuple-element.11.refs_0_), channel_id=1, source_target_pairs={{0,8},{1,9},{2,10},{3,11},{4,12},{5,13},{6,14},{7,15},{8,0},{9,1},... | collective-permute-start | bytes 393224 | tf_op jit(solution)/shard_map/ppermute | solution.py:37
  10.2 9.0 %collective-permute-start.10 = (bf16[128,512]{1,0:T(8,128)(2,1)}, bf16[128,512]{1,0:T(8,128)(2,1)S(1)}, u32[]{:S(2)}, u32[]{:S(2)}) collective-permute-start(bf16[128,512]{1,0:T(8,128)(2,1)} %get-tuple-element.11.refs_0_), channel_id=1, source_target_pairs={{0,1},{1,0},{2,3},{3,2},{4,5},{5,4},{6,7},{7,6},{8,9},{9,8},{10,11... | collective-permute-start | bytes 393224 | tf_op jit(solution)/shard_map/ppermute | solution.py:37
  10.2 9.0 %collective-permute-start.7 = (bf16[128,512]{1,0:T(8,128)(2,1)}, bf16[128,512]{1,0:T(8,128)(2,1)S(1)}, u32[]{:S(2)}, u32[]{:S(2)}) collective-permute-start(bf16[128,512]{1,0:T(8,128)(2,1)} %get-tuple-element.11.refs_0_), channel_id=1, source_target_pairs={{0,2},{1,3},{2,0},{3,1},{4,6},{5,7},{6,4},{7,5},{8,10},{9,11},{10,... | collective-permute-start | bytes 393224 | tf_op jit(solution)/shard_map/ppermute | solution.py:37
  14.6 6.3 %collective-permute-start.14 = (bf16[128,512]{1,0:T(8,128)(2,1)S(1)}, bf16[128,512]{1,0:T(8,128)(2,1)S(1)}, u32[]{:S(2)}, u32[]{:S(2)}) collective-permute-start(bf16[128,512]{1,0:T(8,128)(2,1)S(1)} %collective-permute-done.9.refs_4_), channel_id=1, source_target_pairs={{0,1},{1,0},{2,3},{3,2},{4,5},{5,4},{6,7},{7,6},{8,9},{9,8},{10,11... | collective-permute-start | bytes 393224 | tf_op jit(solution)/shard_map/ppermute | solution.py:37
  16.7 4.1 %collective-permute-start.13 = (bf16[128,512]{1,0:T(8,128)(2,1)S(1)}, bf16[128,512]{1,0:T(8,128)(2,1)S(1)}, u32[]{:S(2)}, u32[]{:S(2)}) collective-permute-start(bf16[128,512]{1,0:T(8,128)(2,1)S(1)} %collective-permute-done.8.refs_3_), channel_id=1, source_target_pairs={{0,1},{1,0},{2,3},{3,2},{4,5},{5,4},{6,7},{7,6},{8,9},{9,8},{10,11... | collective-permute-start | bytes 393224 | tf_op jit(solution)/shard_map/ppermute | solution.py:37
  16.7 7.3 %collective-permute-start.3 = (bf16[128,512]{1,0:T(8,128)(2,1)S(1)}, bf16[128,512]{1,0:T(8,128)(2,1)S(1)}, u32[]{:S(2)}, u32[]{:S(2)}) collective-permute-start(bf16[128,512]{1,0:T(8,128)(2,1)S(1)} %collective-permute-done.refs_1_), channel_id=1, source_target_pairs={{0,6},{1,7},{2,4},{3,5},{4,2},{5,3},{6,0},{7,1},{8,14},{9,15},{10,... | collective-permute-start | bytes 393224 | tf_op jit(solution)/shard_map/ppermute | solution.py:37
  19.2 6.0 %collective-permute-start.2 = (bf16[128,512]{1,0:T(8,128)(2,1)S(1)}, bf16[128,512]{1,0:T(8,128)(2,1)S(1)}, u32[]{:S(2)}, u32[]{:S(2)}) collective-permute-start(bf16[128,512]{1,0:T(8,128)(2,1)S(1)} %collective-permute-done.refs_1_), channel_id=1, source_target_pairs={{0,4},{1,5},{2,6},{3,7},{4,0},{5,1},{6,2},{7,3},{8,12},{9,13},{10,... | collective-permute-start | bytes 393224 | tf_op jit(solution)/shard_map/ppermute | solution.py:37
  19.3 7.0 %collective-permute-start.1 = (bf16[128,512]{1,0:T(8,128)(2,1)S(1)}, bf16[128,512]{1,0:T(8,128)(2,1)S(1)}, u32[]{:S(2)}, u32[]{:S(2)}) collective-permute-start(bf16[128,512]{1,0:T(8,128)(2,1)S(1)} %collective-permute-done.refs_1_), channel_id=1, source_target_pairs={{0,2},{1,3},{2,0},{3,1},{4,6},{5,7},{6,4},{7,5},{8,10},{9,11},{10,... | collective-permute-start | bytes 393224 | tf_op jit(solution)/shard_map/ppermute | solution.py:37
  20.8 9.9 %collective-permute-start.12 = (bf16[128,512]{1,0:T(8,128)(2,1)S(1)}, bf16[128,512]{1,0:T(8,128)(2,1)S(1)}, u32[]{:S(2)}, u32[]{:S(2)}) collective-permute-start(bf16[128,512]{1,0:T(8,128)(2,1)S(1)} %collective-permute-done.7.refs_2_), channel_id=1, source_target_pairs={{0,1},{1,0},{2,3},{3,2},{4,5},{5,4},{6,7},{7,6},{8,9},{9,8},{10,11... | collective-permute-start | bytes 393224 | tf_op jit(solution)/shard_map/ppermute | solution.py:37
  20.8 9.9 %collective-permute-start.11 = (bf16[128,512]{1,0:T(8,128)(2,1)S(1)}, bf16[128,512]{1,0:T(8,128)(2,1)S(1)}, u32[]{:S(2)}, u32[]{:S(2)}) collective-permute-start(bf16[128,512]{1,0:T(8,128)(2,1)S(1)} %collective-permute-done.refs_1_), channel_id=1, source_target_pairs={{0,1},{1,0},{2,3},{3,2},{4,5},{5,4},{6,7},{7,6},{8,9},{9,8},{10,11... | collective-permute-start | bytes 393224 | tf_op jit(solution)/shard_map/ppermute | solution.py:37
  24.0 10.4 %collective-permute-start.6 = (bf16[128,512]{1,0:T(8,128)(2,1)S(1)}, bf16[128,512]{1,0:T(8,128)(2,1)S(1)}, u32[]{:S(2)}, u32[]{:S(2)}) collective-permute-start(bf16[128,512]{1,0:T(8,128)(2,1)S(1)} %collective-permute-done.3.refs_2_), channel_id=1, source_target_pairs={{0,1},{1,0},{2,3},{3,2},{4,5},{5,4},{6,7},{7,6},{8,9},{9,8},{10,11... | collective-permute-start | bytes 393224 | tf_op jit(solution)/shard_map/ppermute | solution.py:37
  25.2 9.1 %collective-permute-start.5 = (bf16[128,512]{1,0:T(8,128)(2,1)S(1)}, bf16[128,512]{1,0:T(8,128)(2,1)S(1)}, u32[]{:S(2)}, u32[]{:S(2)}) collective-permute-start(bf16[128,512]{1,0:T(8,128)(2,1)S(1)} %collective-permute-done.2.refs_1_), channel_id=1, source_target_pairs={{0,1},{1,0},{2,3},{3,2},{4,5},{5,4},{6,7},{7,6},{8,9},{9,8},{10,11... | collective-permute-start | bytes 393224 | tf_op jit(solution)/shard_map/ppermute | solution.py:37
  26.3 8.1 %collective-permute-start.4 = (bf16[128,512]{1,0:T(8,128)(2,1)S(1)}, bf16[128,512]{1,0:T(8,128)(2,1)S(1)}, u32[]{:S(2)}, u32[]{:S(2)}) collective-permute-start(bf16[128,512]{1,0:T(8,128)(2,1)S(1)} %collective-permute-done.1.refs_0_), channel_id=1, source_target_pairs={{0,1},{1,0},{2,3},{3,2},{4,5},{5,4},{6,7},{7,6},{8,9},{9,8},{10,11... | collective-permute-start | bytes 393224 | tf_op jit(solution)/shard_map/ppermute | solution.py:37
where the time goes:
time: 38.3 us; the launch traced here: 38.2 us
  Pallas kernels  14.8 us (39%)
  starting transfers between devices  12.3 us (32%)
  waiting for transfers between devices  10.9 us (28%)
    ppermute x15, starting transfers between devices, partner(): lax.ppermute(x, 'ctx', [(i, i ^ offset) for i in range(lax.axis_size('ctx...  12.3 us
    ppermute x15, waiting for transfers between devices, partner(): lax.ppermute(x, 'ctx', [(i, i ^ offset) for i in range(lax.axis_size('ctx...  10.9 us
    pallas_call x2, Pallas kernels, attend(): pl.pallas_call(functools.partial(attention_kernel, devices, offsets, not...  7.31 us
    pallas_call x1, Pallas kernels, body(): pl.pallas_call(query_kernel, out_shape=jax.ShapeDtypeStruct((rows, HEADS...  4.43 us
    pallas_call x1, Pallas kernels, body(): pl.pallas_call(key_value_kernel, out_shape=(jax.ShapeDtypeStruct((rows, s...  3.1 us
  transfers between devices with their start and end apart: 15, of which 5 were waited for; matrix products, arithmetic and copies ran while one was open for 0% of the time, Pallas kernels for 21%

commit v1 on v0

--- a/solution.py
+++ b/solution.py
@@ -18,7 +18,7 @@
 THETA = 1000000.0
 SCALE = HEAD**-0.5 * math.log2(math.e)
 HIDDEN = -1e30
-UNIT = 4
+UNIT = 2
 TILE = 512
 
 
@@ -304,8 +304,8 @@
         each(b_units, step_b)
         if last:
             for late in range(2):
-                blended = accum[head, late] / jnp.sum(total[head, late], axis=0, keepdims=True)
-                blended = blended.T.astype(BF16)
+                blended = accum[head, late] * (1.0 / jnp.sum(total[head, late], axis=0, keepdims=True))
+                blended = blended.astype(BF16).T
                 for g in range(GROUP):
                     column = (head * GROUP + g) * HEAD
                     out[query_rows[late], column : column + HEAD] = blended[g * half : (g + 1) * half]

time: 38.3 us -> 37.5 us (0.979)
  Pallas kernels: 14.8 us -> 14 us
    pallas_call x2, Pallas kernels: 7.31 us -> 6.51 us  [attend(): pl.pallas_call(functools.partial(attention_kernel, devices, offsets, not...]
  transfers between devices with their start and end apart: 15 -> 15, of which waited for: 5 -> 5; matrix products, arithmetic and copies ran while one was open for 0% -> 0% of each run, Pallas kernels for 21% -> 20%
where the time goes in v1:
time: 37.5 us; the launch traced here: 37.3 us
  Pallas kernels  14 us (37%)
  starting transfers between devices  12.3 us (33%)
  waiting for transfers between devices  10.9 us (29%)
    ppermute x15, starting transfers between devices, partner(): lax.ppermute(x, 'ctx', [(i, i ^ offset) for i in range(lax.axis_size('ctx...  12.3 us
    ppermute x15, waiting for transfers between devices, partner(): lax.ppermute(x, 'ctx', [(i, i ^ offset) for i in range(lax.axis_size('ctx...  10.9 us
    pallas_call x2, Pallas kernels, attend(): pl.pallas_call(functools.partial(attention_kernel, devices, offsets, not...  6.51 us
    pallas_call x1, Pallas kernels, body(): pl.pallas_call(query_kernel, out_shape=jax.ShapeDtypeStruct((rows, HEADS...  4.43 us
    pallas_call x1, Pallas kernels, body(): pl.pallas_call(key_value_kernel, out_shape=(jax.ShapeDtypeStruct((rows, s...  3.1 us
  transfers between devices with their start and end apart: 15, of which 5 were waited for; matrix products, arithmetic and copies ran while one was open for 0% of the time, Pallas kernels for 20%

profile of v1, /device:TPU:0, one launch (start us, length us, event | category | flops | bytes accessed | tf_op | source)
XLA Modules:
  0.0 37.3 jit_solution(17652919098530427289)
XLA Ops:
  0.0 0.0 copy-start
  0.0 3.1 %key_value.1 = (bf16[128,2816]{1,0:T(8,128)(2,1)}, bf16[128,512]{1,0:T(8,128)(2,1)}) custom-call(s32[2,16]{1,0:T(2,128)} %bitcast.4, bf16[128,2048]{1,0:T(8,128)(2,1)} %hidden_in.1, f32[1,2048]{1,0:T(1,128)} %bitcast.7, bf16[2048,256]{1,0:T(8,128)(2,1)} %w_key_in.1, bf16[2048,256]{1,0:T(8,128)(2,1)} %w_value_in.1, f32[1,128]{1,0:T(1,128)} %bitcast.8, ...), custom_call_target="tpu_custom_call" | custom-call | tf_op jit(solution)/shard_map/key_value/pallas_call | solution.py:365
  3.1 0.0 copy-start.1
  3.1 4.1 %collective-permute-start.9 = (bf16[128,512]{1,0:T(8,128)(2,1)}, bf16[128,512]{1,0:T(8,128)(2,1)S(1)}, u32[]{:S(2)}, u32[]{:S(2)}) collective-permute-start(bf16[128,512]{1,0:T(8,128)(2,1)} %get-tuple-element.11.refs_0_), channel_id=1, source_target_pairs={{0,6},{1,7},{2,4},{3,5},{4,2},{5,3},{6,0},{7,1},{8,14},{9,15},{10,... | collective-permute-start | bytes 393224 | tf_op jit(solution)/shard_map/ppermute | solution.py:37
  7.2 0.5 %collective-permute-start.8 = (bf16[128,512]{1,0:T(8,128)(2,1)}, bf16[128,512]{1,0:T(8,128)(2,1)S(1)}, u32[]{:S(2)}, u32[]{:S(2)}) collective-permute-start(bf16[128,512]{1,0:T(8,128)(2,1)} %get-tuple-element.11.refs_0_), channel_id=1, source_target_pairs={{0,4},{1,5},{2,6},{3,7},{4,0},{5,1},{6,2},{7,3},{8,12},{9,13},{10,... | collective-permute-start | bytes 393224 | tf_op jit(solution)/shard_map/ppermute | solution.py:37
  7.6 2.6 %collective-permute-start = (bf16[128,512]{1,0:T(8,128)(2,1)}, bf16[128,512]{1,0:T(8,128)(2,1)S(1)}, u32[]{:S(2)}, u32[]{:S(2)}) collective-permute-start(bf16[128,512]{1,0:T(8,128)(2,1)} %get-tuple-element.11.refs_0_), channel_id=1, source_target_pairs={{0,8},{1,9},{2,10},{3,11},{4,12},{5,13},{6,14},{7,15},{8,0},{9,1},... | collective-permute-start | bytes 393224 | tf_op jit(solution)/shard_map/ppermute | solution.py:37
  10.2 0.0 collective-permute-start.10
  10.2 0.5 %collective-permute-start.7 = (bf16[128,512]{1,0:T(8,128)(2,1)}, bf16[128,512]{1,0:T(8,128)(2,1)S(1)}, u32[]{:S(2)}, u32[]{:S(2)}) collective-permute-start(bf16[128,512]{1,0:T(8,128)(2,1)} %get-tuple-element.11.refs_0_), channel_id=1, source_target_pairs={{0,2},{1,3},{2,0},{3,1},{4,6},{5,7},{6,4},{7,5},{8,10},{9,11},{10,... | collective-permute-start | bytes 393224 | tf_op jit(solution)/shard_map/ppermute | solution.py:37
  10.7 3.8 %collective-permute-done.9.refs_4_ = bf16[128,512]{1,0:T(8,128)(2,1)S(1)} collective-permute-done((bf16[128,512]{1,0:T(8,128)(2,1)}, bf16[128,512]{1,0:T(8,128)(2,1)S(1)}, u32[]{:S(2)}, u32[]{:S(2)}) %collective-permute-start.9) | collective-permute-done | bytes 131104 | tf_op jit(solution)/shard_map/ppermute | solution.py:37
  14.6 0.0 collective-permute-start.14
  14.6 2.1 %collective-permute-done.8.refs_3_ = bf16[128,512]{1,0:T(8,128)(2,1)S(1)} collective-permute-done((bf16[128,512]{1,0:T(8,128)(2,1)}, bf16[128,512]{1,0:T(8,128)(2,1)S(1)}, u32[]{:S(2)}, u32[]{:S(2)}) %collective-permute-start.8) | collective-permute-done | bytes 131104 | tf_op jit(solution)/shard_map/ppermute | solution.py:37
  16.7 0.0 collective-permute-start.13
  16.7 0.0 collective-permute-done.refs_1_
  16.7 2.5 %collective-permute-start.3 = (bf16[128,512]{1,0:T(8,128)(2,1)S(1)}, bf16[128,512]{1,0:T(8,128)(2,1)S(1)}, u32[]{:S(2)}, u32[]{:S(2)}) collective-permute-start(bf16[128,512]{1,0:T(8,128)(2,1)S(1)} %collective-permute-done.refs_1_), channel_id=1, source_target_pairs={{0,6},{1,7},{2,4},{3,5},{4,2},{5,3},{6,0},{7,1},{8,14},{9,15},{10,... | collective-permute-start | bytes 393224 | tf_op jit(solution)/shard_map/ppermute | solution.py:37
  19.2 0.0 collective-permute-done.10.refs_5_
  19.2 0.1 collective-permute-start.2
  19.3 0.0 collective-permute-done.7.refs_2_
  19.3 1.5 %collective-permute-start.1 = (bf16[128,512]{1,0:T(8,128)(2,1)S(1)}, bf16[128,512]{1,0:T(8,128)(2,1)S(1)}, u32[]{:S(2)}, u32[]{:S(2)}) collective-permute-start(bf16[128,512]{1,0:T(8,128)(2,1)S(1)} %collective-permute-done.refs_1_), channel_id=1, source_target_pairs={{0,2},{1,3},{2,0},{3,1},{4,6},{5,7},{6,4},{7,5},{8,10},{9,11},{10,... | collective-permute-start | bytes 393224 | tf_op jit(solution)/shard_map/ppermute | solution.py:37
  20.8 0.0 collective-permute-done.14.refs_9_
  20.8 0.0 collective-permute-start.12
  20.8 0.0 collective-permute-done.13.refs_8_
  20.8 0.5 %collective-permute-start.11 = (bf16[128,512]{1,0:T(8,128)(2,1)S(1)}, bf16[128,512]{1,0:T(8,128)(2,1)S(1)}, u32[]{:S(2)}, u32[]{:S(2)}) collective-permute-start(bf16[128,512]{1,0:T(8,128)(2,1)S(1)} %collective-permute-done.refs_1_), channel_id=1, source_target_pairs={{0,1},{1,0},{2,3},{3,2},{4,5},{5,4},{6,7},{7,6},{8,9},{9,8},{10,11... | collective-permute-start | bytes 393224 | tf_op jit(solution)/shard_map/ppermute | solution.py:37
  21.3 2.7 %collective-permute-done.3.refs_2_ = bf16[128,512]{1,0:T(8,128)(2,1)S(1)} collective-permute-done((bf16[128,512]{1,0:T(8,128)(2,1)S(1)}, bf16[128,512]{1,0:T(8,128)(2,1)S(1)}, u32[]{:S(2)}, u32[]{:S(2)}) %collective-permute-start.3) | collective-permute-done | bytes 131104 | tf_op jit(solution)/shard_map/ppermute | solution.py:37
  24.0 0.0 collective-permute-start.6
  24.0 1.2 %collective-permute-done.2.refs_1_ = bf16[128,512]{1,0:T(8,128)(2,1)S(1)} collective-permute-done((bf16[128,512]{1,0:T(8,128)(2,1)S(1)}, bf16[128,512]{1,0:T(8,128)(2,1)S(1)}, u32[]{:S(2)}, u32[]{:S(2)}) %collective-permute-start.2) | collective-permute-done | bytes 131104 | tf_op jit(solution)/shard_map/ppermute | solution.py:37
  25.2 0.0 collective-permute-start.5
  25.2 1.1 %collective-permute-done.1.refs_0_ = bf16[128,512]{1,0:T(8,128)(2,1)S(1)} collective-permute-done((bf16[128,512]{1,0:T(8,128)(2,1)S(1)}, bf16[128,512]{1,0:T(8,128)(2,1)S(1)}, u32[]{:S(2)}, u32[]{:S(2)}) %collective-permute-start.1) | collective-permute-done | bytes 131104 | tf_op jit(solution)/shard_map/ppermute | solution.py:37
  26.3 0.0 collective-permute-start.4
  26.3 4.4 %query.1.queries = bf16[128,2048]{1,0:T(8,128)(2,1)S(1)} custom-call(bf16[128,2816]{1,0:T(8,128)(2,1)} %get-tuple-element.10.shared_in, bf16[2048,2048]{1,0:T(8,128)(2,1)} %w_query.1), custom_call_target="tpu_custom_call" | custom-call | flops 1073741824 | bytes 8388608 | tf_op jit(solution)/shard_map/query/pallas_call | solution.py:397
  30.8 0.0 collective-permute-done.12.refs_7_
  30.8 0.0 collective-permute-done.11.refs_6_
  30.8 0.0 copy-done
  30.8 0.0 copy-done.1
  30.8 3.1 %attention.2 = (f32[2,2,8,512]{3,2,1,0:T(8,128)S(1)}, f32[2,2,8,512]{3,2,1,0:T(8,128)S(1)}, f32[2,2,128,512]{3,2,1,0:T(8,128)S(1)}) custom-call(s32[2,16]{1,0:T(2,128)S(1)} %bitcast.5, bf16[128,2048]{1,0:T(8,128)(2,1)S(1)} %query.1.queries, bf16[128,512]{1,0:T(8,128)(2,1)S(1)} %copy-done.1, bf16[128,512]{1,0:T(8,128)(2,1)S(1)} %collective-permute-done.refs_1_, ...), custom_call_target="tpu_custom_call" | custom-call | flops 1342177280 | bytes 524288 | tf_op jit(solution)/shard_map/attention/pallas_call | solution.py:333
  33.9 0.0 collective-permute-done.6.refs_5_
  34.0 0.0 collective-permute-done.5.refs_4_
  34.0 0.0 collective-permute-done.4.refs_3_
  34.0 3.4 %attention.3 = bf16[128,2048]{1,0:T(8,128)(2,1)} custom-call(s32[2,16]{1,0:T(2,128)S(1)} %bitcast.6, bf16[128,2048]{1,0:T(8,128)(2,1)S(1)} %query.1.queries, bf16[128,512]{1,0:T(8,128)(2,1)S(1)} %collective-permute-done.1.refs_0_, bf16[128,512]{1,0:T(8,128)(2,1)S(1)} %collective-permute-done.2.refs_1_, bf16[128,512]{1,0:T(8,128)(2,1)S(1)} %collective-permute-done.3.refs_2_, ...), custom_call_target="tpu_custom_call" | custom-call | flops 805306368 | bytes 524288 | tf_op jit(solution)/shard_map/attention/pallas_call | solution.py:333
Async XLA Ops:
  0.0 30.8 %copy-start = (s32[16,2]{0,1:T(2,128)S(1)}, s32[16,2]{0,1:T(2,128)}, u32[]{:S(2)}) copy-start(s32[16,2]{0,1:T(2,128)} %param.10) | copy-start | bytes 388
  3.1 27.7 %copy-start.1 = (bf16[128,512]{1,0:T(8,128)(2,1)S(1)}, bf16[128,512]{1,0:T(8,128)(2,1)}, u32[]{:S(2)}) copy-start(bf16[128,512]{1,0:T(8,128)(2,1)} %get-tuple-element.11.refs_0_) | copy-start | bytes 393220
  3.1 11.4 %collective-permute-start.9 = (bf16[128,512]{1,0:T(8,128)(2,1)}, bf16[128,512]{1,0:T(8,128)(2,1)S(1)}, u32[]{:S(2)}, u32[]{:S(2)}) collective-permute-start(bf16[128,512]{1,0:T(8,128)(2,1)} %get-tuple-element.11.refs_0_), channel_id=1, source_target_pairs={{0,6},{1,7},{2,4},{3,5},{4,2},{5,3},{6,0},{7,1},{8,14},{9,15},{10,... | collective-permute-start | bytes 393224 | tf_op jit(solution)/shard_map/ppermute | solution.py:37
  7.2 9.5 %collective-permute-start.8 = (bf16[128,512]{1,0:T(8,128)(2,1)}, bf16[128,512]{1,0:T(8,128)(2,1)S(1)}, u32[]{:S(2)}, u32[]{:S(2)}) collective-permute-start(bf16[128,512]{1,0:T(8,128)(2,1)} %get-tuple-element.11.refs_0_), channel_id=1, source_target_pairs={{0,4},{1,5},{2,6},{3,7},{4,0},{5,1},{6,2},{7,3},{8,12},{9,13},{10,... | collective-permute-start | bytes 393224 | tf_op jit(solution)/shard_map/ppermute | solution.py:37
  7.6 9.0 %collective-permute-start = (bf16[128,512]{1,0:T(8,128)(2,1)}, bf16[128,512]{1,0:T(8,128)(2,1)S(1)}, u32[]{:S(2)}, u32[]{:S(2)}) collective-permute-start(bf16[128,512]{1,0:T(8,128)(2,1)} %get-tuple-element.11.refs_0_), channel_id=1, source_target_pairs={{0,8},{1,9},{2,10},{3,11},{4,12},{5,13},{6,14},{7,15},{8,0},{9,1},... | collective-permute-start | bytes 393224 | tf_op jit(solution)/shard_map/ppermute | solution.py:37
  10.2 9.0 %collective-permute-start.10 = (bf16[128,512]{1,0:T(8,128)(2,1)}, bf16[128,512]{1,0:T(8,128)(2,1)S(1)}, u32[]{:S(2)}, u32[]{:S(2)}) collective-permute-start(bf16[128,512]{1,0:T(8,128)(2,1)} %get-tuple-element.11.refs_0_), channel_id=1, source_target_pairs={{0,1},{1,0},{2,3},{3,2},{4,5},{5,4},{6,7},{7,6},{8,9},{9,8},{10,11... | collective-permute-start | bytes 393224 | tf_op jit(solution)/shard_map/ppermute | solution.py:37
  10.2 9.0 %collective-permute-start.7 = (bf16[128,512]{1,0:T(8,128)(2,1)}, bf16[128,512]{1,0:T(8,128)(2,1)S(1)}, u32[]{:S(2)}, u32[]{:S(2)}) collective-permute-start(bf16[128,512]{1,0:T(8,128)(2,1)} %get-tuple-element.11.refs_0_), channel_id=1, source_target_pairs={{0,2},{1,3},{2,0},{3,1},{4,6},{5,7},{6,4},{7,5},{8,10},{9,11},{10,... | collective-permute-start | bytes 393224 | tf_op jit(solution)/shard_map/ppermute | solution.py:37
  14.6 6.3 %collective-permute-start.14 = (bf16[128,512]{1,0:T(8,128)(2,1)S(1)}, bf16[128,512]{1,0:T(8,128)(2,1)S(1)}, u32[]{:S(2)}, u32[]{:S(2)}) collective-permute-start(bf16[128,512]{1,0:T(8,128)(2,1)S(1)} %collective-permute-done.9.refs_4_), channel_id=1, source_target_pairs={{0,1},{1,0},{2,3},{3,2},{4,5},{5,4},{6,7},{7,6},{8,9},{9,8},{10,11... | collective-permute-start | bytes 393224 | tf_op jit(solution)/shard_map/ppermute | solution.py:37
  16.7 4.1 %collective-permute-start.13 = (bf16[128,512]{1,0:T(8,128)(2,1)S(1)}, bf16[128,512]{1,0:T(8,128)(2,1)S(1)}, u32[]{:S(2)}, u32[]{:S(2)}) collective-permute-start(bf16[128,512]{1,0:T(8,128)(2,1)S(1)} %collective-permute-done.8.refs_3_), channel_id=1, source_target_pairs={{0,1},{1,0},{2,3},{3,2},{4,5},{5,4},{6,7},{7,6},{8,9},{9,8},{10,11... | collective-permute-start | bytes 393224 | tf_op jit(solution)/shard_map/ppermute | solution.py:37
  16.7 7.3 %collective-permute-start.3 = (bf16[128,512]{1,0:T(8,128)(2,1)S(1)}, bf16[128,512]{1,0:T(8,128)(2,1)S(1)}, u32[]{:S(2)}, u32[]{:S(2)}) collective-permute-start(bf16[128,512]{1,0:T(8,128)(2,1)S(1)} %collective-permute-done.refs_1_), channel_id=1, source_target_pairs={{0,6},{1,7},{2,4},{3,5},{4,2},{5,3},{6,0},{7,1},{8,14},{9,15},{10,... | collective-permute-start | bytes 393224 | tf_op jit(solution)/shard_map/ppermute | solution.py:37
  19.2 6.0 %collective-permute-start.2 = (bf16[128,512]{1,0:T(8,128)(2,1)S(1)}, bf16[128,512]{1,0:T(8,128)(2,1)S(1)}, u32[]{:S(2)}, u32[]{:S(2)}) collective-permute-start(bf16[128,512]{1,0:T(8,128)(2,1)S(1)} %collective-permute-done.refs_1_), channel_id=1, source_target_pairs={{0,4},{1,5},{2,6},{3,7},{4,0},{5,1},{6,2},{7,3},{8,12},{9,13},{10,... | collective-permute-start | bytes 393224 | tf_op jit(solution)/shard_map/ppermute | solution.py:37
  19.3 7.0 %collective-permute-start.1 = (bf16[128,512]{1,0:T(8,128)(2,1)S(1)}, bf16[128,512]{1,0:T(8,128)(2,1)S(1)}, u32[]{:S(2)}, u32[]{:S(2)}) collective-permute-start(bf16[128,512]{1,0:T(8,128)(2,1)S(1)} %collective-permute-done.refs_1_), channel_id=1, source_target_pairs={{0,2},{1,3},{2,0},{3,1},{4,6},{5,7},{6,4},{7,5},{8,10},{9,11},{10,... | collective-permute-start | bytes 393224 | tf_op jit(solution)/shard_map/ppermute | solution.py:37
  20.8 9.9 %collective-permute-start.12 = (bf16[128,512]{1,0:T(8,128)(2,1)S(1)}, bf16[128,512]{1,0:T(8,128)(2,1)S(1)}, u32[]{:S(2)}, u32[]{:S(2)}) collective-permute-start(bf16[128,512]{1,0:T(8,128)(2,1)S(1)} %collective-permute-done.7.refs_2_), channel_id=1, source_target_pairs={{0,1},{1,0},{2,3},{3,2},{4,5},{5,4},{6,7},{7,6},{8,9},{9,8},{10,11... | collective-permute-start | bytes 393224 | tf_op jit(solution)/shard_map/ppermute | solution.py:37
  20.8 9.9 %collective-permute-start.11 = (bf16[128,512]{1,0:T(8,128)(2,1)S(1)}, bf16[128,512]{1,0:T(8,128)(2,1)S(1)}, u32[]{:S(2)}, u32[]{:S(2)}) collective-permute-start(bf16[128,512]{1,0:T(8,128)(2,1)S(1)} %collective-permute-done.refs_1_), channel_id=1, source_target_pairs={{0,1},{1,0},{2,3},{3,2},{4,5},{5,4},{6,7},{7,6},{8,9},{9,8},{10,11... | collective-permute-start | bytes 393224 | tf_op jit(solution)/shard_map/ppermute | solution.py:37
  24.0 9.9 %collective-permute-start.6 = (bf16[128,512]{1,0:T(8,128)(2,1)S(1)}, bf16[128,512]{1,0:T(8,128)(2,1)S(1)}, u32[]{:S(2)}, u32[]{:S(2)}) collective-permute-start(bf16[128,512]{1,0:T(8,128)(2,1)S(1)} %collective-permute-done.3.refs_2_), channel_id=1, source_target_pairs={{0,1},{1,0},{2,3},{3,2},{4,5},{5,4},{6,7},{7,6},{8,9},{9,8},{10,11... | collective-permute-start | bytes 393224 | tf_op jit(solution)/shard_map/ppermute | solution.py:37
  25.2 8.7 %collective-permute-start.5 = (bf16[128,512]{1,0:T(8,128)(2,1)S(1)}, bf16[128,512]{1,0:T(8,128)(2,1)S(1)}, u32[]{:S(2)}, u32[]{:S(2)}) collective-permute-start(bf16[128,512]{1,0:T(8,128)(2,1)S(1)} %collective-permute-done.2.refs_1_), channel_id=1, source_target_pairs={{0,1},{1,0},{2,3},{3,2},{4,5},{5,4},{6,7},{7,6},{8,9},{9,8},{10,11... | collective-permute-start | bytes 393224 | tf_op jit(solution)/shard_map/ppermute | solution.py:37
  26.3 7.7 %collective-permute-start.4 = (bf16[128,512]{1,0:T(8,128)(2,1)S(1)}, bf16[128,512]{1,0:T(8,128)(2,1)S(1)}, u32[]{:S(2)}, u32[]{:S(2)}) collective-permute-start(bf16[128,512]{1,0:T(8,128)(2,1)S(1)} %collective-permute-done.1.refs_0_), channel_id=1, source_target_pairs={{0,1},{1,0},{2,3},{3,2},{4,5},{5,4},{6,7},{7,6},{8,9},{9,8},{10,11... | collective-permute-start | bytes 393224 | tf_op jit(solution)/shard_map/ppermute | solution.py:37

commit v2 on v1

--- a/solution.py
+++ b/solution.py
@@ -153,12 +153,17 @@
 def attention_kernel(devices, offsets, first, last, spans, queries, *refs):
     blocks = sum(len(group) for group in offsets)
     pieces, refs = refs[: len(offsets)], refs[len(offsets) :]
+    heads = KV_HEADS
+
+    def per_head(refs):
+        return [refs[i * heads : (i + 1) * heads] for i in range(3)]
+
     if not first:
-        (peak_in, total_in, accum_in), refs = refs[:3], refs[3:]
+        (peak_in, total_in, accum_in), refs = per_head(refs), refs[3 * heads :]
     if last:
-        out, peak, total, accum, kv, scores_a, scores_b, packed, sem = refs
-    else:
-        peak, total, accum, kv, scores_a, scores_b, packed, sem = refs
+        out, refs = refs[0], refs[1:]
+    (peak, total, accum), refs = per_head(refs), refs[3 * heads :]
+    kv, scores_a, scores_b, packed, result, sem, put_sems = refs
     has_own = offsets[0][0] == 0
     own = lax.axis_index("ctx")
     half = queries.shape[0] // 2
@@ -213,6 +218,7 @@
         if count <= 8:
             for index in range(count):
                 step(index)
+                yield
         else:
             pl.loop(0, count)(step)
 
@@ -251,42 +257,43 @@
                 column = (head * GROUP + g) * HEAD
                 packed[head, late, g * half : (g + 1) * half, :] = queries[query_rows[late], column : column + HEAD]
             if first:
-                peak[head, late] = jnp.full((8, lanes), HIDDEN, F32)
+                peak[head][late] = jnp.full((8, lanes), HIDDEN, F32)
             else:
-                peak[head, late] = peak_in[head, late]
+                peak[head][late] = peak_in[head][late]
 
         def step_a(index):
             scores = score(head, a_rows(index), 1)
             scores_a[slot(head), a_rows(index), :] = scores
-            peak[head, 1] = jnp.maximum(peak[head, 1], folded(scores, jnp.max))
+            peak[head][1] = jnp.maximum(peak[head][1], folded(scores, jnp.max))
 
         def step_b(index):
             late, ahead, rows = b_unit(index)
             scores = score(head, rows, late)
-            key_at = ahead + lax.broadcasted_iota(jnp.int32, scores.shape, 0)
-            query_at = lax.broadcasted_iota(jnp.int32, scores.shape, 1) % half if has_own else half - 1
-            scores = jnp.where(key_at <= query_at, scores, HIDDEN)
+            key_at = ahead + lax.broadcasted_iota(jnp.int32, (unit, HEAD), 0)
+            query_at = lax.broadcasted_iota(jnp.int32, (unit, HEAD), 1) % half if has_own else half - 1
+            limit = jnp.where(key_at <= query_at, -HIDDEN, HIDDEN)
+            scores = jnp.minimum(scores, jnp.concatenate([limit] * (lanes // HEAD), axis=1))
             scores_b[slot(head), b_rows(index), :] = scores
-            peak[head, late] = jnp.maximum(peak[head, late], folded(scores, jnp.max))
-
-        each(len(a_steps), step_a)
-        each(b_units, step_b)
+            peak[head][late] = jnp.maximum(peak[head][late], folded(scores, jnp.max))
+
+        yield from each(len(a_steps), step_a)
+        yield from each(b_units, step_b)
 
     def blend(head):
         for late in range(2):
-            peak[head, late] = spread(peak[head, late], jnp.max)
+            peak[head][late] = spread(peak[head][late], jnp.max)
             if first:
-                total[head, late] = jnp.zeros((8, lanes), F32)
-                accum[head, late] = jnp.zeros((HEAD, lanes), F32)
+                total[head][late] = jnp.zeros((8, lanes), F32)
+                accum[head][late] = jnp.zeros((HEAD, lanes), F32)
             else:
-                decay = jnp.exp2((peak_in[head, late] - peak[head, late]) * SCALE)
-                total[head, late] = total_in[head, late] * decay
-                accum[head, late] = accum_in[head, late] * decay[:1]
+                decay = jnp.exp2((peak_in[head][late] - peak[head][late]) * SCALE)
+                total[head][late] = total_in[head][late] * decay
+                accum[head][late] = accum_in[head][late] * decay[:1]
 
         def add(scores, late, rows):
-            weights = jnp.exp2((scores - peak[head, late][:1]) * SCALE)
-            total[head, late] += folded(weights, jnp.sum)
-            accum[head, late] += lax.dot_general(
+            weights = jnp.exp2((scores - peak[head][late][:1]) * SCALE)
+            total[head][late] += folded(weights, jnp.sum)
+            accum[head][late] += lax.dot_general(
                 kv[rows, pl.ds((KV_HEADS + head) * HEAD, HEAD)],
                 weights.astype(BF16),
                 (((0,), (0,)), ((), ())),
@@ -300,19 +307,32 @@
             late, _, rows = b_unit(index)
             add(scores_b[slot(head), b_rows(index), :], late, rows)
 
-        each(len(a_steps), step_a)
-        each(b_units, step_b)
+        yield from each(len(a_steps), step_a)
+        yield from each(b_units, step_b)
         if last:
             for late in range(2):
-                blended = accum[head, late] * (1.0 / jnp.sum(total[head, late], axis=0, keepdims=True))
+                blended = accum[head][late] * (1.0 / jnp.sum(total[head][late], axis=0, keepdims=True))
                 blended = blended.astype(BF16).T
                 for g in range(GROUP):
-                    column = (head * GROUP + g) * HEAD
-                    out[query_rows[late], column : column + HEAD] = blended[g * half : (g + 1) * half]
-
-    for step in (find_scores, blend) if scores_a.shape[0] == KV_HEADS else (lambda head: (find_scores(head), blend(head)),):
-        for head in range(KV_HEADS):
-            step(head)
+                    result[head, late, :, g * HEAD : (g + 1) * HEAD] = blended[g * half : (g + 1) * half]
+                columns = pl.ds(head * GROUP * HEAD, GROUP * HEAD)
+                put = pltpu.make_async_copy(
+                    result.at[head, late], out.at[query_rows[late], columns], put_sems.at[2 * head + late]
+                )
+                put.start()
+                puts.append(put)
+                yield
+
+    puts = []
+    if scores_a.shape[0] == heads:
+        order = [step(head) for step in (find_scores, blend) for head in range(heads)]
+    else:
+        order = [step(head) for head in range(heads) for step in (find_scores, blend)]
+    for steps in order:
+        for _ in steps:
+            pass
+    for put in puts:
+        put.wait()
 
 
 def attend(devices, offsets, spans, queries, pieces, state=(), last=True):
@@ -322,14 +342,14 @@
     blocks = sum(len(group) for group in offsets)
     part_rows = -(-blocks // UNIT) * UNIT * half
     b_rows = unit_count(blocks, offsets[0][0] == 0) * UNIT * half
-    shapes = [(KV_HEADS, 2, 8, lanes), (KV_HEADS, 2, 8, lanes), (KV_HEADS, 2, HEAD, lanes)]
+    shapes = [(2, 8, lanes)] * (2 * KV_HEADS) + [(2, HEAD, lanes)] * KV_HEADS
     states = [VMEM(shape, F32) for shape in shapes]
     relayed = len(offsets) == blocks
     slots = KV_HEADS if relayed else 1
     if last:
-        out_shape, out_specs = jax.ShapeDtypeStruct((rows, HEADS * HEAD), BF16), placed(VMEM)
+        out_shape, out_specs = jax.ShapeDtypeStruct((rows, HEADS * HEAD), BF16), placed(pl.ANY)
     else:
-        out_shape, out_specs = [jax.ShapeDtypeStruct(shape, F32) for shape in shapes], [placed(VMEM)] * 3
+        out_shape, out_specs = [jax.ShapeDtypeStruct(shape, F32) for shape in shapes], [placed(VMEM)] * len(shapes)
     return pl.pallas_call(
         functools.partial(attention_kernel, devices, offsets, not state, last),
         out_shape=out_shape,
@@ -343,7 +363,9 @@
             VMEM((slots, blocks * half, lanes), F32),
             VMEM((slots, b_rows, lanes), F32),
             VMEM((KV_HEADS, 2, lanes, HEAD), BF16),
+            VMEM((KV_HEADS, 2, half, GROUP * HEAD) if last else (8, HEAD), BF16),
             DMA,
+            DMA((2 * KV_HEADS,)),
         ],
         compiler_params=pltpu.CompilerParams(vmem_limit_bytes=(20 if relayed else 63) << 20),
         cost_estimate=pl.CostEstimate(

time: 37.5 us -> 37.3 us (level)
  no operation moved by 1% of the time
where the time goes in v2:
time: 37.3 us; the launch traced here: 37.2 us
  Pallas kernels  13.9 us (37%)
  starting transfers between devices  12.3 us (33%)
  waiting for transfers between devices  10.9 us (29%)
    ppermute x15, starting transfers between devices, partner(): lax.ppermute(x, 'ctx', [(i, i ^ offset) for i in range(lax.axis_size('ctx...  12.3 us
    ppermute x15, waiting for transfers between devices, partner(): lax.ppermute(x, 'ctx', [(i, i ^ offset) for i in range(lax.axis_size('ctx...  10.9 us
    pallas_call x2, Pallas kernels, attend(): pl.pallas_call(functools.partial(attention_kernel, devices, offsets, not...  6.36 us
    pallas_call x1, Pallas kernels, body(): pl.pallas_call(query_kernel, out_shape=jax.ShapeDtypeStruct((rows, HEADS...  4.43 us
    pallas_call x1, Pallas kernels, body(): pl.pallas_call(key_value_kernel, out_shape=(jax.ShapeDtypeStruct((rows, s...  3.1 us
  transfers between devices with their start and end apart: 15, of which 5 were waited for; matrix products, arithmetic and copies ran while one was open for 0% of the time, Pallas kernels for 20%

profile of v2, /device:TPU:0, one launch (start us, length us, event | category | flops | bytes accessed | tf_op | source)
XLA Modules:
  0.0 37.2 jit_solution(11670055770773325302)
XLA Ops:
  0.0 0.0 copy-start
  0.0 3.1 %key_value.1 = (bf16[128,2816]{1,0:T(8,128)(2,1)}, bf16[128,512]{1,0:T(8,128)(2,1)}) custom-call(s32[2,16]{1,0:T(2,128)} %bitcast.4, bf16[128,2048]{1,0:T(8,128)(2,1)} %hidden_in.1, f32[1,2048]{1,0:T(1,128)} %bitcast.7, bf16[2048,256]{1,0:T(8,128)(2,1)} %w_key_in.1, bf16[2048,256]{1,0:T(8,128)(2,1)} %w_value_in.1, f32[1,128]{1,0:T(1,128)} %bitcast.8, ...), custom_call_target="tpu_custom_call" | custom-call | tf_op jit(solution)/shard_map/key_value/pallas_call | solution.py:387
  3.1 0.0 copy-start.1
  3.1 4.1 %collective-permute-start.9 = (bf16[128,512]{1,0:T(8,128)(2,1)}, bf16[128,512]{1,0:T(8,128)(2,1)S(1)}, u32[]{:S(2)}, u32[]{:S(2)}) collective-permute-start(bf16[128,512]{1,0:T(8,128)(2,1)} %get-tuple-element.14.refs_0_), channel_id=1, source_target_pairs={{0,6},{1,7},{2,4},{3,5},{4,2},{5,3},{6,0},{7,1},{8,14},{9,15},{10,... | collective-permute-start | bytes 393224 | tf_op jit(solution)/shard_map/ppermute | solution.py:37
  7.2 0.5 %collective-permute-start.8 = (bf16[128,512]{1,0:T(8,128)(2,1)}, bf16[128,512]{1,0:T(8,128)(2,1)S(1)}, u32[]{:S(2)}, u32[]{:S(2)}) collective-permute-start(bf16[128,512]{1,0:T(8,128)(2,1)} %get-tuple-element.14.refs_0_), channel_id=1, source_target_pairs={{0,4},{1,5},{2,6},{3,7},{4,0},{5,1},{6,2},{7,3},{8,12},{9,13},{10,... | collective-permute-start | bytes 393224 | tf_op jit(solution)/shard_map/ppermute | solution.py:37
  7.6 2.6 %collective-permute-start = (bf16[128,512]{1,0:T(8,128)(2,1)}, bf16[128,512]{1,0:T(8,128)(2,1)S(1)}, u32[]{:S(2)}, u32[]{:S(2)}) collective-permute-start(bf16[128,512]{1,0:T(8,128)(2,1)} %get-tuple-element.14.refs_0_), channel_id=1, source_target_pairs={{0,8},{1,9},{2,10},{3,11},{4,12},{5,13},{6,14},{7,15},{8,0},{9,1},... | collective-permute-start | bytes 393224 | tf_op jit(solution)/shard_map/ppermute | solution.py:37
  10.2 0.0 collective-permute-start.10
  10.2 0.5 %collective-permute-start.7 = (bf16[128,512]{1,0:T(8,128)(2,1)}, bf16[128,512]{1,0:T(8,128)(2,1)S(1)}, u32[]{:S(2)}, u32[]{:S(2)}) collective-permute-start(bf16[128,512]{1,0:T(8,128)(2,1)} %get-tuple-element.14.refs_0_), channel_id=1, source_target_pairs={{0,2},{1,3},{2,0},{3,1},{4,6},{5,7},{6,4},{7,5},{8,10},{9,11},{10,... | collective-permute-start | bytes 393224 | tf_op jit(solution)/shard_map/ppermute | solution.py:37
  10.7 3.8 %collective-permute-done.9.refs_4_ = bf16[128,512]{1,0:T(8,128)(2,1)S(1)} collective-permute-done((bf16[128,512]{1,0:T(8,128)(2,1)}, bf16[128,512]{1,0:T(8,128)(2,1)S(1)}, u32[]{:S(2)}, u32[]{:S(2)}) %collective-permute-start.9) | collective-permute-done | bytes 131104 | tf_op jit(solution)/shard_map/ppermute | solution.py:37
  14.6 0.0 collective-permute-start.14
  14.6 2.1 %collective-permute-done.8.refs_3_ = bf16[128,512]{1,0:T(8,128)(2,1)S(1)} collective-permute-done((bf16[128,512]{1,0:T(8,128)(2,1)}, bf16[128,512]{1,0:T(8,128)(2,1)S(1)}, u32[]{:S(2)}, u32[]{:S(2)}) %collective-permute-start.8) | collective-permute-done | bytes 131104 | tf_op jit(solution)/shard_map/ppermute | solution.py:37
  16.7 0.0 collective-permute-start.13
  16.7 0.0 collective-permute-done.refs_1_
  16.7 2.5 %collective-permute-start.3 = (bf16[128,512]{1,0:T(8,128)(2,1)S(1)}, bf16[128,512]{1,0:T(8,128)(2,1)S(1)}, u32[]{:S(2)}, u32[]{:S(2)}) collective-permute-start(bf16[128,512]{1,0:T(8,128)(2,1)S(1)} %collective-permute-done.refs_1_), channel_id=1, source_target_pairs={{0,6},{1,7},{2,4},{3,5},{4,2},{5,3},{6,0},{7,1},{8,14},{9,15},{10,... | collective-permute-start | bytes 393224 | tf_op jit(solution)/shard_map/ppermute | solution.py:37
  19.2 0.0 collective-permute-done.10.refs_5_
  19.2 0.1 collective-permute-start.2
  19.3 0.0 collective-permute-done.7.refs_2_
  19.3 1.5 %collective-permute-start.1 = (bf16[128,512]{1,0:T(8,128)(2,1)S(1)}, bf16[128,512]{1,0:T(8,128)(2,1)S(1)}, u32[]{:S(2)}, u32[]{:S(2)}) collective-permute-start(bf16[128,512]{1,0:T(8,128)(2,1)S(1)} %collective-permute-done.refs_1_), channel_id=1, source_target_pairs={{0,2},{1,3},{2,0},{3,1},{4,6},{5,7},{6,4},{7,5},{8,10},{9,11},{10,... | collective-permute-start | bytes 393224 | tf_op jit(solution)/shard_map/ppermute | solution.py:37
  20.8 0.0 collective-permute-done.14.refs_9_
  20.8 0.0 collective-permute-start.12
  20.8 0.0 collective-permute-done.13.refs_8_
  20.8 0.5 %collective-permute-start.11 = (bf16[128,512]{1,0:T(8,128)(2,1)S(1)}, bf16[128,512]{1,0:T(8,128)(2,1)S(1)}, u32[]{:S(2)}, u32[]{:S(2)}) collective-permute-start(bf16[128,512]{1,0:T(8,128)(2,1)S(1)} %collective-permute-done.refs_1_), channel_id=1, source_target_pairs={{0,1},{1,0},{2,3},{3,2},{4,5},{5,4},{6,7},{7,6},{8,9},{9,8},{10,11... | collective-permute-start | bytes 393224 | tf_op jit(solution)/shard_map/ppermute | solution.py:37
  21.3 2.7 %collective-permute-done.3.refs_2_ = bf16[128,512]{1,0:T(8,128)(2,1)S(1)} collective-permute-done((bf16[128,512]{1,0:T(8,128)(2,1)S(1)}, bf16[128,512]{1,0:T(8,128)(2,1)S(1)}, u32[]{:S(2)}, u32[]{:S(2)}) %collective-permute-start.3) | collective-permute-done | bytes 131104 | tf_op jit(solution)/shard_map/ppermute | solution.py:37
  24.0 0.0 collective-permute-start.6
  24.0 1.2 %collective-permute-done.2.refs_1_ = bf16[128,512]{1,0:T(8,128)(2,1)S(1)} collective-permute-done((bf16[128,512]{1,0:T(8,128)(2,1)S(1)}, bf16[128,512]{1,0:T(8,128)(2,1)S(1)}, u32[]{:S(2)}, u32[]{:S(2)}) %collective-permute-start.2) | collective-permute-done | bytes 131104 | tf_op jit(solution)/shard_map/ppermute | solution.py:37
  25.2 0.0 collective-permute-start.5
  25.2 1.1 %collective-permute-done.1.refs_0_ = bf16[128,512]{1,0:T(8,128)(2,1)S(1)} collective-permute-done((bf16[128,512]{1,0:T(8,128)(2,1)S(1)}, bf16[128,512]{1,0:T(8,128)(2,1)S(1)}, u32[]{:S(2)}, u32[]{:S(2)}) %collective-permute-start.1) | collective-permute-done | bytes 131104 | tf_op jit(solution)/shard_map/ppermute | solution.py:37
  26.3 0.0 collective-permute-start.4
  26.3 4.4 %query.1.queries = bf16[128,2048]{1,0:T(8,128)(2,1)S(1)} custom-call(bf16[128,2816]{1,0:T(8,128)(2,1)} %get-tuple-element.13.shared_in, bf16[2048,2048]{1,0:T(8,128)(2,1)} %w_query.1), custom_call_target="tpu_custom_call" | custom-call | flops 1073741824 | bytes 8388608 | tf_op jit(solution)/shard_map/query/pallas_call | solution.py:419
  30.8 0.0 collective-permute-done.12.refs_7_
  30.8 0.0 collective-permute-done.11.refs_6_
  30.8 0.0 copy-done
  30.8 0.0 copy-done.1
  30.8 3.1 %attention.2 = (f32[2,8,512]{2,1,0:T(8,128)S(1)}, f32[2,8,512]{2,1,0:T(8,128)S(1)}, f32[2,8,512]{2,1,0:T(8,128)S(1)}, f32[2,8,512]{2,1,0:T(8,128)S(1)}, f32[2,12...) custom-call(s32[2,16]{1,0:T(2,128)S(1)} %bitcast.5, bf16[128,2048]{1,0:T(8,128)(2,1)S(1)} %query.1.queries, ...), custom_call_target="tpu_custom_call" | custom-call | flops 1342177280 | bytes 524288 | tf_op jit(solution)/shard_map/attention/pallas_call | solution.py:353
  33.9 0.0 collective-permute-done.6.refs_5_
  33.9 0.0 collective-permute-done.5.refs_4_
  33.9 0.0 collective-permute-done.4.refs_3_
  33.9 3.3 %attention.3 = bf16[128,2048]{1,0:T(8,128)(2,1)} custom-call(s32[2,16]{1,0:T(2,128)S(1)} %bitcast.6, bf16[128,2048]{1,0:T(8,128)(2,1)S(1)} %query.1.queries, bf16[128,512]{1,0:T(8,128)(2,1)S(1)} %collective-permute-done.1.refs_0_, bf16[128,512]{1,0:T(8,128)(2,1)S(1)} %collective-permute-done.2.refs_1_, bf16[128,512]{1,0:T(8,128)(2,1)S(1)} %collective-permute-done.3.refs_2_, ...), custom_call_target="tpu_custom_call" | custom-call | flops 805306368 | bytes 524288 | tf_op jit(solution)/shard_map/attention/pallas_call | solution.py:353
Async XLA Ops:
  0.0 30.8 %copy-start = (s32[16,2]{0,1:T(2,128)S(1)}, s32[16,2]{0,1:T(2,128)}, u32[]{:S(2)}) copy-start(s32[16,2]{0,1:T(2,128)} %param.10) | copy-start | bytes 388
  3.1 27.7 %copy-start.1 = (bf16[128,512]{1,0:T(8,128)(2,1)S(1)}, bf16[128,512]{1,0:T(8,128)(2,1)}, u32[]{:S(2)}) copy-start(bf16[128,512]{1,0:T(8,128)(2,1)} %get-tuple-element.14.refs_0_) | copy-start | bytes 393220
  3.1 11.4 %collective-permute-start.9 = (bf16[128,512]{1,0:T(8,128)(2,1)}, bf16[128,512]{1,0:T(8,128)(2,1)S(1)}, u32[]{:S(2)}, u32[]{:S(2)}) collective-permute-start(bf16[128,512]{1,0:T(8,128)(2,1)} %get-tuple-element.14.refs_0_), channel_id=1, source_target_pairs={{0,6},{1,7},{2,4},{3,5},{4,2},{5,3},{6,0},{7,1},{8,14},{9,15},{10,... | collective-permute-start | bytes 393224 | tf_op jit(solution)/shard_map/ppermute | solution.py:37
  7.2 9.5 %collective-permute-start.8 = (bf16[128,512]{1,0:T(8,128)(2,1)}, bf16[128,512]{1,0:T(8,128)(2,1)S(1)}, u32[]{:S(2)}, u32[]{:S(2)}) collective-permute-start(bf16[128,512]{1,0:T(8,128)(2,1)} %get-tuple-element.14.refs_0_), channel_id=1, source_target_pairs={{0,4},{1,5},{2,6},{3,7},{4,0},{5,1},{6,2},{7,3},{8,12},{9,13},{10,... | collective-permute-start | bytes 393224 | tf_op jit(solution)/shard_map/ppermute | solution.py:37
  7.6 9.0 %collective-permute-start = (bf16[128,512]{1,0:T(8,128)(2,1)}, bf16[128,512]{1,0:T(8,128)(2,1)S(1)}, u32[]{:S(2)}, u32[]{:S(2)}) collective-permute-start(bf16[128,512]{1,0:T(8,128)(2,1)} %get-tuple-element.14.refs_0_), channel_id=1, source_target_pairs={{0,8},{1,9},{2,10},{3,11},{4,12},{5,13},{6,14},{7,15},{8,0},{9,1},... | collective-permute-start | bytes 393224 | tf_op jit(solution)/shard_map/ppermute | solution.py:37
  10.2 9.0 %collective-permute-start.10 = (bf16[128,512]{1,0:T(8,128)(2,1)}, bf16[128,512]{1,0:T(8,128)(2,1)S(1)}, u32[]{:S(2)}, u32[]{:S(2)}) collective-permute-start(bf16[128,512]{1,0:T(8,128)(2,1)} %get-tuple-element.14.refs_0_), channel_id=1, source_target_pairs={{0,1},{1,0},{2,3},{3,2},{4,5},{5,4},{6,7},{7,6},{8,9},{9,8},{10,11... | collective-permute-start | bytes 393224 | tf_op jit(solution)/shard_map/ppermute | solution.py:37
  10.2 9.0 %collective-permute-start.7 = (bf16[128,512]{1,0:T(8,128)(2,1)}, bf16[128,512]{1,0:T(8,128)(2,1)S(1)}, u32[]{:S(2)}, u32[]{:S(2)}) collective-permute-start(bf16[128,512]{1,0:T(8,128)(2,1)} %get-tuple-element.14.refs_0_), channel_id=1, source_target_pairs={{0,2},{1,3},{2,0},{3,1},{4,6},{5,7},{6,4},{7,5},{8,10},{9,11},{10,... | collective-permute-start | bytes 393224 | tf_op jit(solution)/shard_map/ppermute | solution.py:37
  14.6 6.3 %collective-permute-start.14 = (bf16[128,512]{1,0:T(8,128)(2,1)S(1)}, bf16[128,512]{1,0:T(8,128)(2,1)S(1)}, u32[]{:S(2)}, u32[]{:S(2)}) collective-permute-start(bf16[128,512]{1,0:T(8,128)(2,1)S(1)} %collective-permute-done.9.refs_4_), channel_id=1, source_target_pairs={{0,1},{1,0},{2,3},{3,2},{4,5},{5,4},{6,7},{7,6},{8,9},{9,8},{10,11... | collective-permute-start | bytes 393224 | tf_op jit(solution)/shard_map/ppermute | solution.py:37
  16.7 4.1 %collective-permute-start.13 = (bf16[128,512]{1,0:T(8,128)(2,1)S(1)}, bf16[128,512]{1,0:T(8,128)(2,1)S(1)}, u32[]{:S(2)}, u32[]{:S(2)}) collective-permute-start(bf16[128,512]{1,0:T(8,128)(2,1)S(1)} %collective-permute-done.8.refs_3_), channel_id=1, source_target_pairs={{0,1},{1,0},{2,3},{3,2},{4,5},{5,4},{6,7},{7,6},{8,9},{9,8},{10,11... | collective-permute-start | bytes 393224 | tf_op jit(solution)/shard_map/ppermute | solution.py:37
  16.7 7.3 %collective-permute-start.3 = (bf16[128,512]{1,0:T(8,128)(2,1)S(1)}, bf16[128,512]{1,0:T(8,128)(2,1)S(1)}, u32[]{:S(2)}, u32[]{:S(2)}) collective-permute-start(bf16[128,512]{1,0:T(8,128)(2,1)S(1)} %collective-permute-done.refs_1_), channel_id=1, source_target_pairs={{0,6},{1,7},{2,4},{3,5},{4,2},{5,3},{6,0},{7,1},{8,14},{9,15},{10,... | collective-permute-start | bytes 393224 | tf_op jit(solution)/shard_map/ppermute | solution.py:37
  19.2 6.0 %collective-permute-start.2 = (bf16[128,512]{1,0:T(8,128)(2,1)S(1)}, bf16[128,512]{1,0:T(8,128)(2,1)S(1)}, u32[]{:S(2)}, u32[]{:S(2)}) collective-permute-start(bf16[128,512]{1,0:T(8,128)(2,1)S(1)} %collective-permute-done.refs_1_), channel_id=1, source_target_pairs={{0,4},{1,5},{2,6},{3,7},{4,0},{5,1},{6,2},{7,3},{8,12},{9,13},{10,... | collective-permute-start | bytes 393224 | tf_op jit(solution)/shard_map/ppermute | solution.py:37
  19.3 7.0 %collective-permute-start.1 = (bf16[128,512]{1,0:T(8,128)(2,1)S(1)}, bf16[128,512]{1,0:T(8,128)(2,1)S(1)}, u32[]{:S(2)}, u32[]{:S(2)}) collective-permute-start(bf16[128,512]{1,0:T(8,128)(2,1)S(1)} %collective-permute-done.refs_1_), channel_id=1, source_target_pairs={{0,2},{1,3},{2,0},{3,1},{4,6},{5,7},{6,4},{7,5},{8,10},{9,11},{10,... | collective-permute-start | bytes 393224 | tf_op jit(solution)/shard_map/ppermute | solution.py:37
  20.8 9.9 %collective-permute-start.12 = (bf16[128,512]{1,0:T(8,128)(2,1)S(1)}, bf16[128,512]{1,0:T(8,128)(2,1)S(1)}, u32[]{:S(2)}, u32[]{:S(2)}) collective-permute-start(bf16[128,512]{1,0:T(8,128)(2,1)S(1)} %collective-permute-done.7.refs_2_), channel_id=1, source_target_pairs={{0,1},{1,0},{2,3},{3,2},{4,5},{5,4},{6,7},{7,6},{8,9},{9,8},{10,11... | collective-permute-start | bytes 393224 | tf_op jit(solution)/shard_map/ppermute | solution.py:37
  20.8 9.9 %collective-permute-start.11 = (bf16[128,512]{1,0:T(8,128)(2,1)S(1)}, bf16[128,512]{1,0:T(8,128)(2,1)S(1)}, u32[]{:S(2)}, u32[]{:S(2)}) collective-permute-start(bf16[128,512]{1,0:T(8,128)(2,1)S(1)} %collective-permute-done.refs_1_), channel_id=1, source_target_pairs={{0,1},{1,0},{2,3},{3,2},{4,5},{5,4},{6,7},{7,6},{8,9},{9,8},{10,11... | collective-permute-start | bytes 393224 | tf_op jit(solution)/shard_map/ppermute | solution.py:37
  24.0 9.9 %collective-permute-start.6 = (bf16[128,512]{1,0:T(8,128)(2,1)S(1)}, bf16[128,512]{1,0:T(8,128)(2,1)S(1)}, u32[]{:S(2)}, u32[]{:S(2)}) collective-permute-start(bf16[128,512]{1,0:T(8,128)(2,1)S(1)} %collective-permute-done.3.refs_2_), channel_id=1, source_target_pairs={{0,1},{1,0},{2,3},{3,2},{4,5},{5,4},{6,7},{7,6},{8,9},{9,8},{10,11... | collective-permute-start | bytes 393224 | tf_op jit(solution)/shard_map/ppermute | solution.py:37
  25.2 8.7 %collective-permute-start.5 = (bf16[128,512]{1,0:T(8,128)(2,1)S(1)}, bf16[128,512]{1,0:T(8,128)(2,1)S(1)}, u32[]{:S(2)}, u32[]{:S(2)}) collective-permute-start(bf16[128,512]{1,0:T(8,128)(2,1)S(1)} %collective-permute-done.2.refs_1_), channel_id=1, source_target_pairs={{0,1},{1,0},{2,3},{3,2},{4,5},{5,4},{6,7},{7,6},{8,9},{9,8},{10,11... | collective-permute-start | bytes 393224 | tf_op jit(solution)/shard_map/ppermute | solution.py:37
  26.3 7.6 %collective-permute-start.4 = (bf16[128,512]{1,0:T(8,128)(2,1)S(1)}, bf16[128,512]{1,0:T(8,128)(2,1)S(1)}, u32[]{:S(2)}, u32[]{:S(2)}) collective-permute-start(bf16[128,512]{1,0:T(8,128)(2,1)S(1)} %collective-permute-done.1.refs_0_), channel_id=1, source_target_pairs={{0,1},{1,0},{2,3},{3,2},{4,5},{5,4},{6,7},{7,6},{8,9},{9,8},{10,11... | collective-permute-start | bytes 393224 | tf_op jit(solution)/shard_map/ppermute | solution.py:37
